TPU v7x, 32 devices: a whole 2x2x4 slice. The times are simulated.
32 devices in a mesh: gx: 8 (over z, x), gy: 4 (over y, core).
Axes of the slice: x: 2, y: 2, z: 4, core: 2. Of those that a mesh axis runs over, the one named last changes fastest.
Arguments:
- velocity: float32 [3, 64, 256, 128], P(None, 'gx', 'gy'), may hold values from -2 to 3, as said below
- counts: int32 [8, 4, 9], P('gx', 'gy'), may hold values from 1 to 1024, as said below
- src_cell: int32 [8, 4, 9, 1024], P('gx', 'gy'), may hold values from 0 to 65535
- weights: float32 [8, 4, 9, 1024], P('gx', 'gy'), may hold values from 0.05 to 0.35
- dst_cell: int32 [8, 4, 9, 1024], P('gx', 'gy'), may hold values from 0 to 65535
- blade_tile: int32 [20, 192], replicated, may hold values from 0 to 31, as said below
- blade_cell: int32 [20, 192], replicated, may hold values from 0 to 65535
- blade_coef: float32 [20, 192], replicated, may hold values from 0.5 to 2
Outputs:
- updated: float32 [3, 64, 256, 128], P(None, 'gx', 'gy')
- forcing: float32 [3, 64, 256, 128], P(None, 'gx', 'gy')
Inputs may be any that keep to these rules, and one draw needn't show every extreme that they name: The velocity components, streamwise with a mean near 1. `counts`: some list is full, with 1024 used slots. `blade_tile`: turbines stand near one spanwise row of tiles; a turbine's points lie in at most three tiles.
All inputs are finite; a program needn't handle non-finite values.
Results may differ from a plain program's by a relative error of at most 0.00002.
Values sent between devices are 32-bit elements; how exact they have to be, the bound alone decides.
No kernel may reach another device: no remote copies, remote signals or barrier semaphores. Data moves between devices by JAX's collectives and lax.ppermute only.
A program may use at most 256 MiB of HBM per device.

v0:
```python
import jax
import jax.numpy as jnp
from jax import lax
from jax.sharding import PartitionSpec as P


def padded_2(cells, sides, width):
    for axis, dim in sides:
        count = lax.axis_size(axis)
        head = lax.slice_in_dim(cells, 0, width, axis=dim)
        tail = lax.slice_in_dim(cells, cells.shape[dim] - width, cells.shape[dim], axis=dim)
        cells = jnp.concatenate(
            [
                lax.ppermute(tail, axis, [(i, (i + 1) % count) for i in range(count)]),
                cells,
                lax.ppermute(head, axis, [((i + 1) % count, i) for i in range(count)]),
            ],
            axis=dim,
        )
    return cells


def body(velocity, counts, src_cell, weights, dst_cell, blade_tile, blade_cell, blade_coef):
    components = velocity.shape[0]
    cells_x = velocity.shape[1]
    cells_y = velocity.shape[2]
    levels = velocity.shape[3]
    total_cells = cells_x * cells_y * levels
    flat_vel = velocity.reshape(components, total_cells)
    count_y = lax.axis_size("gy")
    index_x = lax.axis_index("gx")
    index_y = lax.axis_index("gy")
    my_tile = index_x * count_y + index_y
    sampled = jnp.take(flat_vel, blade_cell, axis=1)
    owned = (blade_tile == my_tile)[None]
    sampled = jnp.where(owned, sampled, jnp.zeros_like(sampled))
    points = blade_cell.shape[1]
    points_x = lax.psum(sampled[0], ("gx", "gy"))
    rotor_mean = jnp.sum(points_x, axis=1) / points
    forces = -blade_coef[None] * rotor_mean[None, :, None] * sampled
    forcing = (
        jnp.zeros((components, total_cells), jnp.float32)
        .at[:, blade_cell.reshape(-1)]
        .add(forces.reshape(components, -1))
    )
    capacity = src_cell.shape[-1]
    active = lax.broadcasted_iota(jnp.int32, (9, capacity), 1) < counts[0, 0][:, None]
    masked_w = jnp.where(active, weights[0, 0], jnp.zeros_like(weights[0, 0]))
    picked = jnp.take(flat_vel, src_cell[0, 0].reshape(-1), axis=1).reshape(components, 9, capacity)
    blocks = jnp.concatenate([picked * masked_w[None], masked_w[None]], axis=0)
    grid_blocks = blocks.reshape(4, 3, 3, capacity)
    bordered = padded_2(grid_blocks, (("gx", 1), ("gy", 2)), 1)
    arrived = bordered[:, ::-2, ::-2].reshape(4, 9, capacity)
    targets = dst_cell[0, 0].reshape(-1)
    totals = jnp.zeros((4, total_cells), jnp.float32).at[:, targets].add(arrived.reshape(4, -1))
    corrected = (1.0 - totals[3]) * flat_vel - totals[:3]
    field_now = corrected.reshape(components, cells_x, cells_y, levels)
    padded = padded_2(field_now, (("gx", 1), ("gy", 2)), 1)
    padded = jnp.pad(padded, ((0, 0), (0, 0), (0, 0), (1, 1)))
    center = padded[:, 1:-1, 1:-1, 1:-1]
    east_side = padded[:, 2:, 1:-1, 1:-1]
    west_side = padded[:, :-2, 1:-1, 1:-1]
    north_side = padded[:, 1:-1, 2:, 1:-1]
    south_side = padded[:, 1:-1, :-2, 1:-1]
    upper_side = padded[:, 1:-1, 1:-1, 2:]
    lower_side = padded[:, 1:-1, 1:-1, :-2]
    laplace = (
        east_side + west_side + north_side + south_side + upper_side + lower_side - 6.0 * center
    )
    advection = (
        center[0:1] * (east_side - west_side) * 0.5
        + center[1:2] * (north_side - south_side) * 0.5
        + center[2:3] * (upper_side - lower_side) * 0.5
    )
    forcing_field = forcing.reshape(components, cells_x, cells_y, levels)
    updated = center + 0.2 * (0.15 * laplace - advection + forcing_field)
    return (updated, forcing_field)


def solution(mesh):
    placed = (
        P(None, "gx", "gy", None),
        P("gx", "gy", None),
        P("gx", "gy", None, None),
        P("gx", "gy", None, None),
        P("gx", "gy", None, None),
        P(),
        P(),
        P(),
    )
    return jax.shard_map(
        body,
        mesh=mesh,
        in_specs=placed,
        out_specs=(P(None, "gx", "gy", None), P(None, "gx", "gy", None)),
        check_vma=False,
    )
```

profile of v0, /device:TPU:1, one launch (start us, length us, event | category | flops | bytes accessed | tf_op | source)
XLA Modules:
  0.0 389.9 jit_solution(10842976870287354699)
XLA Ops:
  0.6 0.0 copy-start.2
  0.6 17.6 %copy.47 = f32[3,8,64,128]{0,3,2,1:T(8,128)} copy(f32[3,8,64,128]{3,2,1,0:T(8,128)} %param.8) | data formatting | bytes 1572864 | tf_op args[0]
  18.2 0.0 copy-start.7
  18.2 0.0 copy-start.3
  18.2 0.0 copy-start.4
  18.2 0.0 copy-start.1
  18.2 0.0 copy-done.2
  18.3 41.5 %gather_fusion = f32[9216,3]{1,0:T(8,128)} fusion(f32[3,65536]{0,1:T(8,128)} %bitcast.38, s32[9216]{0:T(1024)S(1)} %broadcast_clamp_fusion), kind=kCustom, calls=%fused_computation | custom fusion | bytes 258048 | tf_op jit(solution)/shard_map/jit(_take)/gather | solution.py:49
  59.8 0.0 copy-start.6
  59.8 3.1 copy.48
  62.9 0.1 reduce
  63.0 0.5 broadcast.151
  63.5 0.0 copy-done.7
  63.5 0.7 reduce.15
  64.2 0.1 lt.84
  64.2 0.0 copy-done.3
  64.2 0.1 reduce.2
  64.4 0.1 fusion.15
  64.5 0.1 compare_select_fusion.2
  64.6 0.1 select_multiply_fusion
  64.7 2.1 collective-permute-start
  66.8 3.1 collective-permute-start.1
  69.9 0.0 copy-done.4
  70.0 0.0 copy-done.1
  70.0 0.1 reshape.205
  70.1 16.8 %gather_fusion.1 = f32[3840,3]{1,0:T(8,128)S(1)} fusion(f32[3,65536]{0,1:T(8,128)} %bitcast.39, s32[4096]{0:T(1024)S(1)} %pad_clamp_fusion), kind=kCustom, calls=%fused_computation.1 | custom fusion | bytes 107520 | tf_op jit(solution)/shard_map/jit(_take)/gather | solution.py:34
  86.9 0.9 copy.56
  87.8 0.0 copy-done.6
  87.8 37.7 %psum.7 = f32[20,192]{1,0:T(8,128)S(1)} all-reduce(f32[20,192]{1,0:T(8,128)S(1)} %fusion.17), channel_id=1, replica_groups=mesh['gx'=8,'gy'=4] {'gx','gy'}, use_global_device_ids=true, to_apply=%region_1.2 | all-reduce | flops 3840 | bytes 30720 | tf_op jit(solution)/shard_map/psum | solution.py:38
  125.6 0.1 reduce_sum.9
  125.7 0.0 collective-permute-done
  125.7 0.0 collective-permute-done.1
  125.7 0.1 pad_maximum_fusion.12
  125.8 3.4 collective-permute-start.2
  129.2 0.0 collective-permute-start.3
  129.2 0.0 copy-done.5
  129.2 0.1 negate_multiply_fusion
  129.3 0.1 broadcast_in_dim.75
  129.3 0.1 broadcast_in_dim.77
  129.4 0.1 reshape.193
  129.5 0.1 mul.117
  129.6 1.8 collective-permute-done.2
  131.4 1.6 collective-permute-done.3
  133.0 0.1 pad_maximum_fusion.8
  133.2 3.0 copy.49
  136.2 62.9 %scatter_custom_fusion = f32[4,65536]{0,1:T(8,128)} fusion(s32[9216]{0:T(1024)S(1)} %bitcast.52, f32[9216,4]{1,0:T(8,128)} %copy.49, f32[]{:T(128)} %constant.18.clone.1), kind=kCustom, calls=%fused_computation.12 | custom fusion | flops 36864 | bytes 1049088 | tf_op jit(solution)/shard_map/scatter-add | solution.py:55
  199.1 20.3 %fusion = f32[65536]{0:T(1024)S(1)} fusion(f32[4,65536]{0,1:T(8,128)} %scatter_custom_fusion), kind=kLoop, calls=%fused_computation.9 | loop fusion | flops 65536 | bytes 524288 | tf_op jit(solution)/shard_map/sub | solution.py:56
  219.4 34.2 %slice_subtract_fusion = f32[3,65536]{0,1:T(8,128)} fusion(f32[4,65536]{0,1:T(8,128)} %scatter_custom_fusion, f32[65536]{0:T(1024)S(1)} %fusion, f32[3,8,64,128]{0,3,2,1:T(8,128)} %copy.47), kind=kLoop, calls=%fused_computation.7 | loop fusion | flops 393216 | bytes 2621440 | tf_op jit(solution)/shard_map/sub | solution.py:56
  253.6 19.5 %copy.59 = f32[3,8,64,128]{3,2,1,0:T(8,128)S(1)} copy(f32[3,8,64,128]{0,3,2,1:T(8,128)} %bitcast.37) | data formatting | bytes 1572864 | tf_op jit(solution)/shard_map/reshape | solution.py:57
  273.1 2.8 collective-permute-start.4
  276.0 0.0 collective-permute-start.5
  276.0 37.5 %scatter_custom_fusion.1 = f32[3,65536]{0,1:T(8,128)} fusion(s32[3840]{0:T(1024)S(1)} %fusion.18, f32[]{:T(128)} %constant.18.clone.1, f32[3840,3]{1,0:T(8,128)S(1)} %gather_fusion.1, f32[]{:T(128)} %constant.22.clone.1, f32[3840]{0:T(1024)S(1)} %mul.117, pred[3840]{0:T(1024)(128)(4,1)S(1)} %broadcast_in_dim.77, pred[3840]{0:T(1024)(128)(4,1)S(1)} %broadcast_in_dim.75), kind=kCustom, calls=%fused_computation.10 | custom fusion | flops 46080 | bytes 2778624 | tf_op jit(solution)/shard_map/scatter-add | solution.py:44
  313.5 19.5 %copy.58 = f32[3,8,64,128]{3,2,1,0:T(8,128)S(1)} copy(f32[3,8,64,128]{0,3,2,1:T(8,128)} %bitcast.40) | data formatting | bytes 1572864 | tf_op jit(solution)/shard_map/reshape | solution.py:75
  333.0 0.0 copy-start
  333.0 0.0 collective-permute-done.4
  333.0 0.0 collective-permute-done.5
  333.0 0.1 collective-permute-start.6
  333.1 1.7 collective-permute-start.7
  334.8 52.5 %slice_reduce_fusion.2 = (f32[65536]{0:T(1024)S(1)}, f32[65536]{0:T(1024)S(1)}, f32[65536]{0:T(1024)S(1)}) fusion(f32[3,65536]{0,1:T(8,128)} %slice_subtract_fusion), kind=kLoop, calls=%fused_computation.6 | loop fusion | bytes 1572864 | tf_op jit(solution)/shard_map/slice | solution.py:71
  387.3 0.0 collective-permute-done.6
  387.3 0.0 collective-permute-done.7
  387.3 0.8 select_maximum_fusion
  388.1 0.0 copy-done
  388.1 1.8 multiply_add_fusion
  (18 shorter events, 0.4 us)
Async XLA Ops:
  0.6 17.6 %copy-start.2 = (s32[1,1,9,1024]{3,1,2,0:T(1,128)S(1)}, s32[1,1,9,1024]{3,1,2,0:T(1,128)}, u32[]{:S(2)}) copy-start(s32[1,1,9,1024]{3,1,2,0:T(1,128)} %param.10) | copy-start | bytes 110596
  18.2 45.3 %copy-start.7 = (s32[1,1,9]{2,1,0:T(1,128)S(1)}, s32[1,1,9]{2,1,0:T(1,128)}, u32[]{:S(2)}) copy-start(s32[1,1,9]{2,1,0:T(1,128)} %param.9) | copy-start | bytes 112
  18.2 46.0 %copy-start.3 = (f32[1,1,9,1024]{3,1,2,0:T(1,128)S(1)}, f32[1,1,9,1024]{3,1,2,0:T(1,128)}, u32[]{:S(2)}) copy-start(f32[1,1,9,1024]{3,1,2,0:T(1,128)} %param.11) | copy-start | bytes 110596
  18.2 51.7 %copy-start.4 = (s32[1,1,9,1024]{3,1,2,0:T(1,128)S(1)}, s32[1,1,9,1024]{3,1,2,0:T(1,128)}, u32[]{:S(2)}) copy-start(s32[1,1,9,1024]{3,1,2,0:T(1,128)} %param.12) | copy-start | bytes 110596
  18.2 51.8 %copy-start.1 = (s32[20,192]{1,0:T(8,128)S(1)}, s32[20,192]{1,0:T(8,128)}, u32[]{:S(2)}) copy-start(s32[20,192]{1,0:T(8,128)} %param.14) | copy-start | bytes 46084
  59.8 28.0 %copy-start.6 = (s32[20,192]{1,0:T(8,128)S(1)}, s32[20,192]{1,0:T(8,128)}, u32[]{:S(2)}) copy-start(s32[20,192]{1,0:T(8,128)} %param.13) | copy-start | bytes 46084
  59.8 69.4 %copy-start.5 = (f32[20,192]{1,0:T(8,128)S(1)}, f32[20,192]{1,0:T(8,128)}, u32[]{:S(2)}) copy-start(f32[20,192]{1,0:T(8,128)} %param.15) | copy-start | bytes 46084
  64.7 61.0 %collective-permute-start = (f32[4,1,3,1024]{3,0,2,1:T(4,128)S(1)}, f32[4,1,3,1024]{3,0,2,1:T(4,128)S(1)}, u32[]{:S(2)}, u32[]{:S(2)}) collective-permute-start(f32[4,1,3,1024]{3,0,2,1:T(4,128)S(1)} %get-tuple-element.19), channel_id=1, source_target_pairs={{0,4},{4,8},{8,12},{12,16},{16,20},{20,24},{24,28},{28,0},{1,5},{5... | collective-permute-start | bytes 147464 | tf_op jit(solution)/shard_map/ppermute | solution.py:14
  66.8 58.9 %collective-permute-start.1 = (f32[4,1,3,1024]{3,0,2,1:T(4,128)S(1)}, f32[4,1,3,1024]{3,0,2,1:T(4,128)S(1)}, u32[]{:S(2)}, u32[]{:S(2)}) collective-permute-start(f32[4,1,3,1024]{3,0,2,1:T(4,128)S(1)} %get-tuple-element.20), channel_id=1, source_target_pairs={{4,0},{8,4},{12,8},{16,12},{20,16},{24,20},{28,24},{0,28},{5,1},{9... | collective-permute-start | bytes 147464 | tf_op jit(solution)/shard_map/ppermute | solution.py:16
  125.8 5.6 %collective-permute-start.2 = (f32[4,5,1,1024]{3,0,2,1:T(4,128)S(1)}, f32[4,5,1,1024]{3,0,2,1:T(4,128)S(1)}, u32[]{:S(2)}, u32[]{:S(2)}) collective-permute-start(f32[4,5,1,1024]{3,0,2,1:T(4,128)S(1)} %get-tuple-element.17), channel_id=1, source_target_pairs={{0,1},{1,2},{2,3},{3,0},{4,5},{5,6},{6,7},{7,4},{8,9},{9,10},{10,1... | collective-permute-start | bytes 245768 | tf_op jit(solution)/shard_map/ppermute | solution.py:14
  129.2 3.9 collective-permute-start.3
  273.1 59.8 %collective-permute-start.4 = (f32[3,1,64,128]{3,2,1,0:T(8,128)S(1)}, f32[3,1,64,128]{3,2,1,0:T(8,128)S(1)}, u32[]{:S(2)}, u32[]{:S(2)}) collective-permute-start(f32[3,1,64,128]{3,2,1,0:T(8,128)S(1)} %get-tuple-element.16), channel_id=1, source_target_pairs={{4,0},{8,4},{12,8},{16,12},{20,16},{24,20},{28,24},{0,28},{5,1},{9... | collective-permute-start | bytes 294920 | tf_op jit(solution)/shard_map/ppermute | solution.py:16
  276.0 57.0 %collective-permute-start.5 = (f32[3,1,64,128]{3,2,1,0:T(8,128)S(1)}, f32[3,1,64,128]{3,2,1,0:T(8,128)S(1)}, u32[]{:S(2)}, u32[]{:S(2)}) collective-permute-start(f32[3,1,64,128]{3,2,1,0:T(8,128)S(1)} %get-tuple-element.15), channel_id=1, source_target_pairs={{0,4},{4,8},{8,12},{12,16},{16,20},{20,24},{24,28},{28,0},{1,5},{5... | collective-permute-start | bytes 294920 | tf_op jit(solution)/shard_map/ppermute | solution.py:14
  333.0 55.2 %copy-start = (f32[3,8,64,128]{3,2,1,0:T(8,128)}, f32[3,8,64,128]{3,2,1,0:T(8,128)S(1)}, u32[]{:S(2)}) copy-start(f32[3,8,64,128]{3,2,1,0:T(8,128)S(1)} %copy.58) | copy-start | bytes 2359300
  333.0 54.3 %collective-permute-start.6 = (f32[3,10,1,128]{3,2,1,0:T(1,128)S(1)}, f32[3,10,1,128]{3,2,1,0:T(1,128)S(1)}, u32[]{:S(2)}, u32[]{:S(2)}) collective-permute-start(f32[3,10,1,128]{3,2,1,0:T(1,128)S(1)} %get-tuple-element.14), channel_id=1, source_target_pairs={{1,0},{2,1},{3,2},{0,3},{5,4},{6,5},{7,6},{4,7},{9,8},{10,9},{11,1... | collective-permute-start | bytes 46088 | tf_op jit(solution)/shard_map/ppermute | solution.py:16
  333.1 54.2 %collective-permute-start.7 = (f32[3,10,1,128]{3,2,1,0:T(1,128)S(1)}, f32[3,10,1,128]{3,2,1,0:T(1,128)S(1)}, u32[]{:S(2)}, u32[]{:S(2)}) collective-permute-start(f32[3,10,1,128]{3,2,1,0:T(1,128)S(1)} %get-tuple-element.13), channel_id=1, source_target_pairs={{0,1},{1,2},{2,3},{3,0},{4,5},{5,6},{6,7},{7,4},{8,9},{9,10},{10,1... | collective-permute-start | bytes 46088 | tf_op jit(solution)/shard_map/ppermute | solution.py:14
where the time goes:
time: 391 us; the launch traced here: 390 us
  local copies, waits for them, and re-layouts  175 us (45%)
  other arithmetic  159 us (41%)
  blocking collectives  37.7 us (10%)
  starting transfers between devices  13.2 us (3%)
    scatter-add x1, other arithmetic, body(): jnp.zeros((4, total_cells), jnp.float32).at[:, targets]  62.9 us
    sub x2, other arithmetic, body(): corrected = (1.0 - totals[3]) * flat_vel - totals[:3]  54.5 us
    slice x1, local copies, waits for them, and re-layouts, body(): center[0:1] * (east_side - west_side) * 0.5  52.5 us
    gather x2, local copies, waits for them, and re-layouts, body(): jnp.take(flat_vel, src_cell[0, 0].reshape(-1), axis=1)  44.6 us
    psum x1, blocking collectives, body(): points_x = lax.psum(sampled[0], ('gx', 'gy'))  37.7 us
    scatter-add x1, other arithmetic, body(): forcing = jnp.zeros((components, total_cells), jnp.float32).at[:, blade_c...  37.5 us
    reshape x1, local copies, waits for them, and re-layouts, body(): field_now = corrected.reshape(components, cells_x, cells_y, levels)  19.5 us
    reshape x1, local copies, waits for them, and re-layouts, body(): forcing_field = forcing.reshape(components, cells_x, cells_y, levels)  19.5 us
  transfers between devices with their start and end apart: 8, of which 2 were waited for; matrix products, arithmetic and copies ran while one was open for 33% of the time, Pallas kernels for 0%

commit v1 on v0

--- a/solution.py
+++ b/solution.py
@@ -35,7 +35,7 @@
     owned = (blade_tile == my_tile)[None]
     sampled = jnp.where(owned, sampled, jnp.zeros_like(sampled))
     points = blade_cell.shape[1]
-    points_x = lax.psum(sampled[0], ("gx", "gy"))
+    points_x = lax.psum(lax.psum(sampled[0], "gy"), "gx")
     rotor_mean = jnp.sum(points_x, axis=1) / points
     forces = -blade_coef[None] * rotor_mean[None, :, None] * sampled
     forcing = (

time: 391 us -> 396 us (1.013)
  starting transfers between devices: 13.2 us -> 17.5 us
    ppermute x4, starting transfers between devices: 7.2 us -> 14.3 us  [padded_2(): lax.ppermute(tail, axis, [(i, (i + 1) % count) for i in range(count)])]
    psum x1 -> x2, blocking collectives: 37.7 us -> 38.3 us  [body(): points_x = lax.psum(lax.psum(sampled[0], 'gy'), 'gx')]
  transfers between devices with their start and end apart: 8 -> 8, of which waited for: 2 -> 2; matrix products, arithmetic and copies ran while one was open for 33% -> 32% of each run, Pallas kernels for 0% -> 0%
where the time goes in v1:
time: 396 us; the launch traced here: 395 us
  local copies, waits for them, and re-layouts  175 us (44%)
  other arithmetic  159 us (40%)
  blocking collectives  38.3 us (10%)
  starting transfers between devices  17.5 us (4%)
    scatter-add x1, other arithmetic, body(): jnp.zeros((4, total_cells), jnp.float32).at[:, targets]  62.9 us
    sub x2, other arithmetic, body(): corrected = (1.0 - totals[3]) * flat_vel - totals[:3]  54.5 us
    slice x1, local copies, waits for them, and re-layouts, body(): center[0:1] * (east_side - west_side) * 0.5  52.5 us
    gather x2, local copies, waits for them, and re-layouts, body(): jnp.take(flat_vel, src_cell[0, 0].reshape(-1), axis=1)  44.6 us
    psum x2, blocking collectives, body(): points_x = lax.psum(lax.psum(sampled[0], 'gy'), 'gx')  38.3 us
    scatter-add x1, other arithmetic, body(): forcing = jnp.zeros((components, total_cells), jnp.float32).at[:, blade_c...  37.5 us
    reshape x1, local copies, waits for them, and re-layouts, body(): field_now = corrected.reshape(components, cells_x, cells_y, levels)  19.5 us
    reshape x1, local copies, waits for them, and re-layouts, body(): forcing_field = forcing.reshape(components, cells_x, cells_y, levels)  19.5 us
  transfers between devices with their start and end apart: 8, of which 2 were waited for; matrix products, arithmetic and copies ran while one was open for 32% of the time, Pallas kernels for 0%

profile of v1, /device:TPU:1, one launch (start us, length us, event | category | flops | bytes accessed | tf_op | source)
XLA Modules:
  0.0 394.8 jit_solution(8664108280674274974)
XLA Ops:
  0.6 0.0 copy-start.2
  0.6 17.6 %copy.47 = f32[3,8,64,128]{0,3,2,1:T(8,128)} copy(f32[3,8,64,128]{3,2,1,0:T(8,128)} %param.8) | data formatting | bytes 1572864 | tf_op args[0]
  18.2 0.0 copy-start.7
  18.2 0.0 copy-start.3
  18.2 0.0 copy-start.4
  18.2 0.0 copy-start.1
  18.2 0.0 copy-done.2
  18.3 41.5 %gather_fusion = f32[9216,3]{1,0:T(8,128)} fusion(f32[3,65536]{0,1:T(8,128)} %bitcast.38, s32[9216]{0:T(1024)S(1)} %broadcast_clamp_fusion), kind=kCustom, calls=%fused_computation | custom fusion | bytes 258048 | tf_op jit(solution)/shard_map/jit(_take)/gather | solution.py:49
  59.8 3.1 copy.48
  62.9 0.1 reduce
  63.0 0.5 broadcast.151
  63.5 0.0 copy-done.7
  63.5 0.7 reduce.15
  64.2 0.1 lt.84
  64.2 0.0 copy-done.3
  64.2 0.1 reduce.2
  64.4 0.1 fusion.15
  64.5 0.1 compare_select_fusion.2
  64.6 0.1 select_multiply_fusion
  64.7 2.1 collective-permute-start
  66.8 3.1 collective-permute-start.1
  69.9 0.0 copy-done.4
  70.0 0.0 copy-done.1
  70.0 0.1 reshape.205
  70.1 16.8 %gather_fusion.1 = f32[3840,3]{1,0:T(8,128)S(1)} fusion(f32[3,65536]{0,1:T(8,128)} %bitcast.39, s32[4096]{0:T(1024)S(1)} %pad_clamp_fusion), kind=kCustom, calls=%fused_computation.1 | custom fusion | bytes 107520 | tf_op jit(solution)/shard_map/jit(_take)/gather | solution.py:34
  86.9 0.9 copy.56
  87.8 0.0 copy-done.6
  87.8 10.8 %psum.14 = f32[20,192]{1,0:T(8,128)S(1)} all-reduce(f32[20,192]{1,0:T(8,128)S(1)} %fusion.17), channel_id=1, replica_groups=mesh['gx'=8,'gy'=4] {'gy'}, use_global_device_ids=true, to_apply=%region_1.2 | all-reduce | flops 3840 | bytes 30720 | tf_op jit(solution)/shard_map/psum | solution.py:38
  98.6 27.5 %psum.15 = f32[20,192]{1,0:T(8,128)S(1)} all-reduce(f32[20,192]{1,0:T(8,128)S(1)} %psum.14), channel_id=1, replica_groups=mesh['gx'=8,'gy'=4] {'gx'}, use_global_device_ids=true, to_apply=%region_2.3 | all-reduce | flops 3840 | bytes 30720 | tf_op jit(solution)/shard_map/psum | solution.py:38
  126.1 0.1 reduce_sum.9
  126.3 0.0 collective-permute-done
  126.3 0.0 collective-permute-done.1
  126.3 0.1 pad_maximum_fusion.12
  126.4 9.0 %collective-permute-start.2 = (f32[4,5,1,1024]{3,0,2,1:T(4,128)S(1)}, f32[4,5,1,1024]{3,0,2,1:T(4,128)S(1)}, u32[]{:S(2)}, u32[]{:S(2)}) collective-permute-start(f32[4,5,1,1024]{3,0,2,1:T(4,128)S(1)} %get-tuple-element.17), channel_id=1, source_target_pairs={{0,1},{1,2},{2,3},{3,0},{4,5},{5,6},{6,7},{7,4},{8,9},{9,10},{10,1... | collective-permute-start | bytes 245768 | tf_op jit(solution)/shard_map/ppermute | solution.py:14
  135.3 0.0 collective-permute-start.3
  135.4 0.0 copy-done.5
  135.4 0.1 negate_multiply_fusion
  135.4 0.1 broadcast_in_dim.75
  135.5 0.1 broadcast_in_dim.77
  135.6 0.1 reshape.193
  135.7 0.1 mul.117
  135.8 1.1 collective-permute-done.2
  136.8 2.4 collective-permute-done.3
  139.2 0.1 pad_maximum_fusion.8
  139.4 3.0 copy.49
  142.4 62.9 %scatter_custom_fusion = f32[4,65536]{0,1:T(8,128)} fusion(s32[9216]{0:T(1024)S(1)} %bitcast.52, f32[9216,4]{1,0:T(8,128)} %copy.49, f32[]{:T(128)} %constant.18.clone.1), kind=kCustom, calls=%fused_computation.12 | custom fusion | flops 36864 | bytes 1049088 | tf_op jit(solution)/shard_map/scatter-add | solution.py:55
  205.3 20.3 %fusion = f32[65536]{0:T(1024)S(1)} fusion(f32[4,65536]{0,1:T(8,128)} %scatter_custom_fusion), kind=kLoop, calls=%fused_computation.9 | loop fusion | flops 65536 | bytes 524288 | tf_op jit(solution)/shard_map/sub | solution.py:56
  225.6 34.2 %slice_subtract_fusion = f32[3,65536]{0,1:T(8,128)} fusion(f32[4,65536]{0,1:T(8,128)} %scatter_custom_fusion, f32[65536]{0:T(1024)S(1)} %fusion, f32[3,8,64,128]{0,3,2,1:T(8,128)} %copy.47), kind=kLoop, calls=%fused_computation.7 | loop fusion | flops 393216 | bytes 2621440 | tf_op jit(solution)/shard_map/sub | solution.py:56
  259.8 19.5 %copy.59 = f32[3,8,64,128]{3,2,1,0:T(8,128)S(1)} copy(f32[3,8,64,128]{0,3,2,1:T(8,128)} %bitcast.37) | data formatting | bytes 1572864 | tf_op jit(solution)/shard_map/reshape | solution.py:57
  279.3 0.1 collective-permute-start.4
  279.4 1.5 collective-permute-start.5
  280.9 37.5 %scatter_custom_fusion.1 = f32[3,65536]{0,1:T(8,128)} fusion(s32[3840]{0:T(1024)S(1)} %fusion.18, f32[]{:T(128)} %constant.18.clone.1, f32[3840,3]{1,0:T(8,128)S(1)} %gather_fusion.1, f32[]{:T(128)} %constant.22.clone.1, f32[3840]{0:T(1024)S(1)} %mul.117, pred[3840]{0:T(1024)(128)(4,1)S(1)} %broadcast_in_dim.77, pred[3840]{0:T(1024)(128)(4,1)S(1)} %broadcast_in_dim.75), kind=kCustom, calls=%fused_computation.10 | custom fusion | flops 46080 | bytes 2778624 | tf_op jit(solution)/shard_map/scatter-add | solution.py:44
  318.3 19.5 %copy.58 = f32[3,8,64,128]{3,2,1,0:T(8,128)S(1)} copy(f32[3,8,64,128]{0,3,2,1:T(8,128)} %bitcast.40) | data formatting | bytes 1572864 | tf_op jit(solution)/shard_map/reshape | solution.py:75
  337.8 0.0 copy-start
  337.8 0.0 collective-permute-done.4
  337.8 0.0 collective-permute-done.5
  337.9 0.1 collective-permute-start.6
  337.9 1.7 collective-permute-start.7
  339.7 52.5 %slice_reduce_fusion.2 = (f32[65536]{0:T(1024)S(1)}, f32[65536]{0:T(1024)S(1)}, f32[65536]{0:T(1024)S(1)}) fusion(f32[3,65536]{0,1:T(8,128)} %slice_subtract_fusion), kind=kLoop, calls=%fused_computation.6 | loop fusion | bytes 1572864 | tf_op jit(solution)/shard_map/slice | solution.py:71
  392.2 0.0 collective-permute-done.6
  392.2 0.0 collective-permute-done.7
  392.2 0.8 select_maximum_fusion
  393.0 0.0 copy-done
  393.0 1.8 multiply_add_fusion
  (19 shorter events, 0.4 us)
Async XLA Ops:
  0.6 17.6 %copy-start.2 = (s32[1,1,9,1024]{3,1,2,0:T(1,128)S(1)}, s32[1,1,9,1024]{3,1,2,0:T(1,128)}, u32[]{:S(2)}) copy-start(s32[1,1,9,1024]{3,1,2,0:T(1,128)} %param.10) | copy-start | bytes 110596
  18.2 45.3 %copy-start.7 = (s32[1,1,9]{2,1,0:T(1,128)S(1)}, s32[1,1,9]{2,1,0:T(1,128)}, u32[]{:S(2)}) copy-start(s32[1,1,9]{2,1,0:T(1,128)} %param.9) | copy-start | bytes 112
  18.2 46.0 %copy-start.3 = (f32[1,1,9,1024]{3,1,2,0:T(1,128)S(1)}, f32[1,1,9,1024]{3,1,2,0:T(1,128)}, u32[]{:S(2)}) copy-start(f32[1,1,9,1024]{3,1,2,0:T(1,128)} %param.11) | copy-start | bytes 110596
  18.2 51.7 %copy-start.4 = (s32[1,1,9,1024]{3,1,2,0:T(1,128)S(1)}, s32[1,1,9,1024]{3,1,2,0:T(1,128)}, u32[]{:S(2)}) copy-start(s32[1,1,9,1024]{3,1,2,0:T(1,128)} %param.12) | copy-start | bytes 110596
  18.2 51.8 %copy-start.1 = (s32[20,192]{1,0:T(8,128)S(1)}, s32[20,192]{1,0:T(8,128)}, u32[]{:S(2)}) copy-start(s32[20,192]{1,0:T(8,128)} %param.14) | copy-start | bytes 46084
  59.8 28.0 %copy-start.6 = (s32[20,192]{1,0:T(8,128)S(1)}, s32[20,192]{1,0:T(8,128)}, u32[]{:S(2)}) copy-start(s32[20,192]{1,0:T(8,128)} %param.13) | copy-start | bytes 46084
  59.8 75.6 %copy-start.5 = (f32[20,192]{1,0:T(8,128)S(1)}, f32[20,192]{1,0:T(8,128)}, u32[]{:S(2)}) copy-start(f32[20,192]{1,0:T(8,128)} %param.15) | copy-start | bytes 46084
  64.7 61.5 %collective-permute-start = (f32[4,1,3,1024]{3,0,2,1:T(4,128)S(1)}, f32[4,1,3,1024]{3,0,2,1:T(4,128)S(1)}, u32[]{:S(2)}, u32[]{:S(2)}) collective-permute-start(f32[4,1,3,1024]{3,0,2,1:T(4,128)S(1)} %get-tuple-element.19), channel_id=1, source_target_pairs={{0,4},{4,8},{8,12},{12,16},{16,20},{20,24},{24,28},{28,0},{1,5},{5... | collective-permute-start | bytes 147464 | tf_op jit(solution)/shard_map/ppermute | solution.py:14
  66.8 59.4 %collective-permute-start.1 = (f32[4,1,3,1024]{3,0,2,1:T(4,128)S(1)}, f32[4,1,3,1024]{3,0,2,1:T(4,128)S(1)}, u32[]{:S(2)}, u32[]{:S(2)}) collective-permute-start(f32[4,1,3,1024]{3,0,2,1:T(4,128)S(1)} %get-tuple-element.20), channel_id=1, source_target_pairs={{4,0},{8,4},{12,8},{16,12},{20,16},{24,20},{28,24},{0,28},{5,1},{9... | collective-permute-start | bytes 147464 | tf_op jit(solution)/shard_map/ppermute | solution.py:16
  126.4 10.5 %collective-permute-start.2 = (f32[4,5,1,1024]{3,0,2,1:T(4,128)S(1)}, f32[4,5,1,1024]{3,0,2,1:T(4,128)S(1)}, u32[]{:S(2)}, u32[]{:S(2)}) collective-permute-start(f32[4,5,1,1024]{3,0,2,1:T(4,128)S(1)} %get-tuple-element.17), channel_id=1, source_target_pairs={{0,1},{1,2},{2,3},{3,0},{4,5},{5,6},{6,7},{7,4},{8,9},{9,10},{10,1... | collective-permute-start | bytes 245768 | tf_op jit(solution)/shard_map/ppermute | solution.py:14
  135.3 3.9 collective-permute-start.3
  279.3 58.5 %collective-permute-start.4 = (f32[3,1,64,128]{3,2,1,0:T(8,128)S(1)}, f32[3,1,64,128]{3,2,1,0:T(8,128)S(1)}, u32[]{:S(2)}, u32[]{:S(2)}) collective-permute-start(f32[3,1,64,128]{3,2,1,0:T(8,128)S(1)} %get-tuple-element.16), channel_id=1, source_target_pairs={{4,0},{8,4},{12,8},{16,12},{20,16},{24,20},{28,24},{0,28},{5,1},{9... | collective-permute-start | bytes 294920 | tf_op jit(solution)/shard_map/ppermute | solution.py:16
  279.4 58.5 %collective-permute-start.5 = (f32[3,1,64,128]{3,2,1,0:T(8,128)S(1)}, f32[3,1,64,128]{3,2,1,0:T(8,128)S(1)}, u32[]{:S(2)}, u32[]{:S(2)}) collective-permute-start(f32[3,1,64,128]{3,2,1,0:T(8,128)S(1)} %get-tuple-element.15), channel_id=1, source_target_pairs={{0,4},{4,8},{8,12},{12,16},{16,20},{20,24},{24,28},{28,0},{1,5},{5... | collective-permute-start | bytes 294920 | tf_op jit(solution)/shard_map/ppermute | solution.py:14
  337.8 55.2 %copy-start = (f32[3,8,64,128]{3,2,1,0:T(8,128)}, f32[3,8,64,128]{3,2,1,0:T(8,128)S(1)}, u32[]{:S(2)}) copy-start(f32[3,8,64,128]{3,2,1,0:T(8,128)S(1)} %copy.58) | copy-start | bytes 2359300
  337.9 54.3 %collective-permute-start.6 = (f32[3,10,1,128]{3,2,1,0:T(1,128)S(1)}, f32[3,10,1,128]{3,2,1,0:T(1,128)S(1)}, u32[]{:S(2)}, u32[]{:S(2)}) collective-permute-start(f32[3,10,1,128]{3,2,1,0:T(1,128)S(1)} %get-tuple-element.14), channel_id=1, source_target_pairs={{1,0},{2,1},{3,2},{0,3},{5,4},{6,5},{7,6},{4,7},{9,8},{10,9},{11,1... | collective-permute-start | bytes 46088 | tf_op jit(solution)/shard_map/ppermute | solution.py:16
  337.9 54.2 %collective-permute-start.7 = (f32[3,10,1,128]{3,2,1,0:T(1,128)S(1)}, f32[3,10,1,128]{3,2,1,0:T(1,128)S(1)}, u32[]{:S(2)}, u32[]{:S(2)}) collective-permute-start(f32[3,10,1,128]{3,2,1,0:T(1,128)S(1)} %get-tuple-element.13), channel_id=1, source_target_pairs={{0,1},{1,2},{2,3},{3,0},{4,5},{5,6},{6,7},{7,4},{8,9},{9,10},{10,1... | collective-permute-start | bytes 46088 | tf_op jit(solution)/shard_map/ppermute | solution.py:14
